TPU v7x, 32 devices: a whole 2x2x4 slice. The times are simulated.
32 devices in a mesh: sample: 4 (over y, x), fsdp: 8 (over z, core).
Axes of the slice: x: 2, y: 2, z: 4, core: 2. Of those that a mesh axis runs over, the one named last changes fastest.
Arguments:
- seed_step: int32 [2], replicated, may hold values from 0 to 16777215
- attn: bfloat16 [16384, 2048], P(('sample', 'fsdp')), may hold values from -6 to 6
- resid: bfloat16 [16384, 4096], P(('sample', 'fsdp')), may hold values from -36 to 36
- cotangent: bfloat16 [16384, 4096], P(('sample', 'fsdp')), may hold values from -6 to 6
- gain: bfloat16 [4096], replicated, may hold values from 0.099609375 to 1.8984375
- mean: float32 [2048, 4096], P('fsdp'), may hold values from -6 to 6
- hess: float32 [2048, 4096], P('fsdp'), may hold values from 0.25 to 4
- momentum: float32 [2048, 4096], P('fsdp'), may hold values from -3 to 3
Outputs:
- new_mean: float32 [2048, 4096], P('fsdp')
- new_hess: float32 [2048, 4096], P('fsdp')
- new_momentum: float32 [2048, 4096], P('fsdp')
All inputs are finite; a program needn't handle non-finite values.
Results may differ from a plain program's by a relative error of at most 0.0035.
Values may be sent and summed in bfloat16 or wider, within the bound.
A program may use at most 192 MiB of HBM per device.

v0:
```python
import jax
import jax.numpy as jnp
from jax import lax
from jax.sharding import PartitionSpec as P

ess_value = 10.0
decay_first = 0.8
decay_second = 0.8
step_size = 0.3
damping = 0.1
norm_eps = 1e-05


def noise_table(seed_step, group_id, row_start, row_count, in_width, width):
    row_index = jnp.arange(row_count, dtype=jnp.int32)[:, None] + row_start
    col_index = jnp.arange(width, dtype=jnp.int32)[None, :]
    mixing = (group_id * in_width + row_index) * width + col_index
    mixing = jnp.bitwise_xor(mixing, seed_step[0])
    mixing = mixing * 668265261 + seed_step[1] * 374761393
    mixing = jnp.bitwise_xor(mixing, jnp.right_shift(mixing, 15) & 131071)
    mixing = mixing * 739982445
    mixing = jnp.bitwise_xor(mixing, jnp.right_shift(mixing, 12) & 1048575)
    mixing = mixing * 695872825
    mixing = jnp.bitwise_xor(mixing, jnp.right_shift(mixing, 15) & 131071)
    first_unif = ((mixing & 4095).astype(jnp.float32) + 0.5) / 4096.0
    second_unif = ((jnp.right_shift(mixing, 12) & 4095).astype(jnp.float32) + 0.5) / 4096.0
    return 2.449489742783178 * (first_unif + second_unif - 1.0)


def ivon_update(mean, hess, momentum, grad_sum, curv_sum, groups):
    grad_mean = grad_sum / groups
    hess_est = curv_sum / groups
    new_momentum = decay_first * momentum + (1.0 - decay_first) * grad_mean
    new_hess = (
        decay_second * hess
        + (1.0 - decay_second) * hess_est
        + 0.5 * (1.0 - decay_second) ** 2 * (hess - hess_est) ** 2 / (hess + damping)
    )
    new_mean = mean - step_size * (new_momentum + damping * mean) / (new_hess + damping)
    return (new_mean, new_hess, new_momentum)


def per_device(seed_step, attn, resid, cotangent, gain, mean, hess, momentum):
    own_rows = mean.shape[0]
    width = mean.shape[1]
    in_width = attn.shape[1]
    scaling = in_width ** (-0.5)
    groups = lax.axis_size("sample")
    group_id = lax.axis_index("sample")
    shard_id = lax.axis_index("fsdp")
    sigma = 1.0 / jnp.sqrt(ess_value * (hess + damping))
    epsilon = noise_table(seed_step, group_id, shard_id * own_rows, own_rows, in_width, width)
    sampled = (
        mean.astype(jnp.bfloat16).astype(jnp.float32)
        + sigma.astype(jnp.bfloat16).astype(jnp.float32) * epsilon
    ).astype(jnp.bfloat16)
    columns = attn
    product = jnp.dot(
        columns,
        lax.all_gather(sampled, "fsdp", axis=0, tiled=True),
        preferred_element_type=jnp.float32,
    )
    total = resid.astype(jnp.float32) + product * scaling
    inverse = lax.rsqrt(jnp.mean(total * total, axis=-1, keepdims=True) + norm_eps)
    upstream = gain.astype(jnp.float32)[None, :] * cotangent.astype(jnp.float32)
    back = inverse * upstream - total * inverse**3 * jnp.mean(
        total * upstream, axis=-1, keepdims=True
    )
    back_low = back.astype(jnp.bfloat16)
    columns = attn
    grad = lax.psum_scatter(
        (
            lax.dot_general(
                columns, back_low, (((0,), (0,)), ((), ())), preferred_element_type=jnp.float32
            )
            * scaling
        ).astype(jnp.bfloat16),
        "fsdp",
        scatter_dimension=0,
        tiled=True,
    ).astype(jnp.float32)
    curvature = grad * epsilon / sigma
    grad_sum, curv_sum = (
        lax.psum(grad.astype(jnp.bfloat16), "sample").astype(jnp.float32),
        lax.psum(curvature.astype(jnp.bfloat16), "sample").astype(jnp.float32),
    )
    return ivon_update(mean, hess, momentum, grad_sum, curv_sum, groups)


def solution(mesh):
    placed = (
        P(),
        P(("sample", "fsdp"), None),
        P(("sample", "fsdp"), None),
        P(("sample", "fsdp"), None),
        P(),
        P("fsdp", None),
        P("fsdp", None),
        P("fsdp", None),
    )
    return jax.shard_map(
        per_device,
        mesh=mesh,
        in_specs=placed,
        out_specs=(P("fsdp", None), P("fsdp", None), P("fsdp", None)),
        check_vma=False,
    )
```

profile of v0, /device:TPU:0, one launch (start us, length us, event | category | flops | bytes accessed | tf_op | source)
XLA Modules:
  0.0 530.1 jit_solution(14531092193861123255)
XLA Ops:
  7.2 0.0 copy-start
  7.2 0.0 all-gather.2.cloned.1.call-start
  7.2 1.4 fusion.13
  8.6 5.6 %copy.14 = f32[256,4096]{0,1:T(8,128)} copy(f32[256,4096]{1,0:T(8,128)} %param.14) | data formatting | bytes 8388608 | tf_op args[6]
  14.2 5.6 %copy.19 = f32[256,4096]{0,1:T(8,128)} copy(f32[256,4096]{1,0:T(8,128)} %param.13) | data formatting | bytes 8388608 | tf_op args[5]
  20.5 0.0 copy-start.2
  20.5 7.9 %add_convert_fusion = bf16[256,4096]{0,1:T(8,128)(2,1)} fusion(f32[256,4096]{0,1:T(8,128)} %copy.14, s32[]{:T(128)} %bitcast.1, s32[]{:T(128)} %bitcast, s32[256]{0:T(256)S(1)} %add_multiply_fusion.1, f32[256,4096]{0,1:T(8,128)} %copy.19), kind=kLoop, calls=%fused_computation.22 | loop fusion | flops 36700160 | bytes 10486792 | tf_op jit(solution)/shard_map/convert_element_type | solution.py:56
  28.4 0.0 all-gather.2.cloned.1.call-update
  28.4 0.2 reduce-scatter.2.cloned.1.call-start
  28.6 0.0 copy-done.2
  28.7 6.4 %copy.15 = bf16[512,4096]{0,1:T(8,128)(2,1)} copy(bf16[512,4096]{1,0:T(8,128)(2,1)} %param.11) | data formatting | bytes 8388608 | tf_op args[3]
  35.1 6.6 %copy.12 = bf16[512,4096]{0,1:T(8,128)(2,1)} copy(bf16[512,4096]{1,0:T(8,128)(2,1)} %param.10) | data formatting | bytes 8388608 | tf_op args[2]
  41.6 141.4 %all-gather.2.cloned.1.call-done = bf16[2048,4096]{0,1:T(8,128)(2,1)} async-done(((bf16[256,4096]{0,1:T(8,128)(2,1)}), bf16[2048,4096]{0,1:T(8,128)(2,1)}) %all-gather.2.cloned.1.call-update) | async-done | bytes 16777232 | tf_op jit(solution)/shard_map/all_gather | solution.py:60
  183.1 0.0 copy-done
  183.1 17.4 %multiply_reduce_fusion.1 = (f32[512]{0:T(512)S(1)}, f32[512]{0:T(512)S(1)}, f32[512,4096]{0,1:T(8,128)}) fusion(bf16[512,4096]{0,1:T(8,128)(2,1)} %copy.15, f32[4096]{0:T(1024)S(1)} %convert_element_type.60, bf16[2048,4096]{0,1:T(8,128)(2,1)} %all-gather.2.cloned.1.call-done, bf16[512,2048]{1,0:T(8,128)(2,1)S(1)} %copy-done, bf16[512,4096]{0,1:T(8,128)(2,1)} %copy.12), kind=kOutput, calls=%fused_computation.6 | convolution fusion | flops 8608808960 | bytes 35672064 | tf_op jit(solution)/shard_map/dot_general | solution.py:58
  200.5 18.1 %fusion = bf16[2048,4096]{0,1:T(8,128)(2,1)} fusion(bf16[512,2048]{1,0:T(8,128)(2,1)S(1)} %copy-done, f32[512,4096]{0,1:T(8,128)} %get-tuple-element.17, bf16[512,4096]{0,1:T(8,128)(2,1)} %copy.15, f32[512]{0:T(512)S(1)} %get-tuple-element.18, f32[512]{0:T(512)S(1)} %get-tuple-element.14, f32[4096]{0:T(1024)S(1)} %convert_element_type.60, ...), kind=kOutput, calls=%fused_computation.1 | convolution fusion | flops 8621391872 | bytes 31479808 | tf_op jit(solution)/shard_map/dot_general | solution.py:73
  218.6 0.0 reduce-scatter.2.cloned.1.call-update
  218.6 0.3 all-reduce.3.cloned.1.call-start
  218.9 166.3 %reduce-scatter.2.cloned.1.call-done = bf16[256,4096]{0,1:T(8,128)(2,1)} async-done(((bf16[2048,4096]{0,1:T(8,128)(2,1)}), bf16[256,4096]{0,1:T(8,128)(2,1)}) %reduce-scatter.2.cloned.1.call-update) | async-done | bytes 2097168 | tf_op jit(solution)/shard_map/reduce_scatter | solution.py:71
  385.2 7.8 %divide_convert_fusion = bf16[256,4096]{0,1:T(8,128)(2,1)} fusion(bf16[256,4096]{0,1:T(8,128)(2,1)} %reduce-scatter.2.cloned.1.call-done, f32[256,4096]{0,1:T(8,128)} %copy.14, s32[]{:T(128)} %bitcast.1, s32[]{:T(128)} %bitcast, s32[256]{0:T(256)S(1)} %add_multiply_fusion.1), kind=kLoop, calls=%fused_computation.16 | loop fusion | flops 33554432 | bytes 8389640 | tf_op jit(solution)/shard_map/convert_element_type | solution.py:85
  393.0 0.0 all-reduce.3.cloned.1.call-update
  393.0 5.6 %copy.11 = f32[256,4096]{0,1:T(8,128)} copy(f32[256,4096]{1,0:T(8,128)} %param.15) | data formatting | bytes 8388608 | tf_op args[7]
  398.7 97.1 %all-reduce.3.cloned.1.call-done = (bf16[256,4096]{0,1:T(8,128)(2,1)}, bf16[256,4096]{0,1:T(8,128)(2,1)}) async-done(((bf16[256,4096]{0,1:T(8,128)(2,1)}, bf16[256,4096]{0,1:T(8,128)(2,1)}), (bf16[256,4096]{0,1:T(8,128)(2,1)}, bf16[256,4096]{0,1:T(8,128)(2,1)})) %all-reduce.3.cloned.1.call-update) | async-done | bytes 4194320 | tf_op jit(solution)/shard_map/psum | solution.py:85
  495.7 10.9 %divide_subtract_fusion = (f32[256,4096]{0,1:T(8,128)}, f32[256,4096]{0,1:T(8,128)}, f32[256,4096]{0,1:T(8,128)}) fusion(f32[256,4096]{0,1:T(8,128)} %copy.19, bf16[256,4096]{0,1:T(8,128)(2,1)} %get-tuple-element.9, f32[256,4096]{0,1:T(8,128)} %copy.11, f32[256,4096]{0,1:T(8,128)} %copy.14, bf16[256,4096]{0,1:T(8,128)(2,1)} %get-tuple-element.8), kind=kLoop, calls=%fused_computation.15 | loop fusion | flops 22020096 | bytes 29360128 | tf_op jit(solution)/shard_map/sub | solution.py:39
  506.6 5.6 %copy.20 = f32[256,4096]{1,0:T(8,128)} copy(f32[256,4096]{0,1:T(8,128)} %get-tuple-element.10) | data formatting | bytes 8388608
  512.2 5.6 %copy.22 = f32[256,4096]{1,0:T(8,128)} copy(f32[256,4096]{0,1:T(8,128)} %get-tuple-element.11) | data formatting | bytes 8388608
  517.8 0.0 copy-start.1
  517.8 5.7 %copy.21 = f32[256,4096]{1,0:T(8,128)} copy(f32[256,4096]{0,1:T(8,128)} %get-tuple-element.12) | data formatting | bytes 8388608
  523.5 0.0 copy-done.1
  (3 shorter events, 0.0 us)
Async XLA Ops:
  7.2 175.9 %copy-start = (bf16[512,2048]{1,0:T(8,128)(2,1)S(1)}, bf16[512,2048]{1,0:T(8,128)(2,1)}, u32[]{:S(2)}) copy-start(bf16[512,2048]{1,0:T(8,128)(2,1)} %param.9) | copy-start | bytes 6291460
  7.2 175.9 %all-gather.2.cloned.1.call-start = ((), (), s32[]{:S(2)}) async-start(), calls=%async_computation.1 | async-start | bytes 18874368 | tf_op jit(solution)/shard_map/all_gather | solution.py:60
  20.5 8.2 %copy-start.2 = (bf16[4096]{0:T(1024)(128)(2,1)S(1)}, bf16[4096]{0:T(1024)(128)(2,1)}, u32[]{:S(2)}) copy-start(bf16[4096]{0:T(1024)(128)(2,1)} %param.12) | copy-start | bytes 24580
  28.4 356.8 %reduce-scatter.2.cloned.1.call-start = ((), (), s32[]{:S(2)}) async-start(), calls=%async_computation.2 | async-start | bytes 18874368 | tf_op jit(solution)/shard_map/reduce_scatter | solution.py:71
  218.6 277.2 %all-reduce.3.cloned.1.call-start = ((), (), s32[]{:S(2)}) async-start(), calls=%async_computation.3 | async-start | bytes 8388608 | tf_op jit(solution)/shard_map/psum | solution.py:85
  517.8 5.7 %copy-start.1 = (bf16[512,2048]{1,0:T(8,128)(2,1)S(1)}, bf16[512,2048]{1,0:T(8,128)(2,1)}, u32[]{:S(2)}) copy-start(bf16[512,2048]{1,0:T(8,128)(2,1)} %param.9) | copy-start | bytes 6291460
Sparse Core Ops, SparseCore 0:
  28.5 154.5 all-gather.1
  218.7 166.4 reduce-scatter.1
  393.2 102.5 all-reduce.2
where the time goes:
time: 531 us; the launch traced here: 530 us
  waiting for transfers between devices  405 us (76%)
  local copies, waits for them, and re-layouts  48.1 us (9%)
  matrix products  35.5 us (7%)
  other arithmetic  26.6 us (5%)
  between operations  14.4 us (3%)
    reduce_scatter x1, waiting for transfers between devices, per_device(): lax.psum_scatter((lax.dot_general(columns, back_low, (((0,), (0,)), ((),...  166 us
    all_gather x1, waiting for transfers between devices, per_device(): lax.all_gather(sampled, 'fsdp', axis=0, tiled=True)  141 us
    psum x1, waiting for transfers between devices, per_device(): lax.psum(curvature.astype(jnp.bfloat16), 'sample').astype(jnp.float32)  97.1 us
    unnamed x14, local copies, waits for them, and re-layouts  46.7 us
    dot_general x1, matrix products, per_device(): lax.dot_general(columns, back_low, (((0,), (0,)), ((), ())), preferred_el...  18.1 us
    dot_general x1, matrix products, per_device(): jnp.dot(columns, lax.all_gather(sampled, 'fsdp', axis=0, tiled=True), pre...  17.4 us
    sub x1, other arithmetic, ivon_update(): mean - step_size * (new_momentum + damping * mean) / (new_hess + damping)  10.9 us
  transfers between devices with their start and end apart: 3, of which 3 were waited for; matrix products, arithmetic and copies ran while one was open for 4% of the time, Pallas kernels for 0%

commit v1 on v0

v1 whole, which is shorter than its diff:
```python
import jax
import jax.numpy as jnp
from jax import lax
from jax.experimental.layout import Layout, with_layout_constraint
from jax.sharding import PartitionSpec as P

ess_value = 10.0
decay_first = 0.8
decay_second = 0.8
step_size = 0.3
damping = 0.1
norm_eps = 1e-05


def noise_table(seed_step, group_id, row_start, row_count, in_width, width, col_start, col_count):
    row_index = jnp.arange(row_count, dtype=jnp.int32)[:, None] + row_start
    col_index = jnp.arange(col_count, dtype=jnp.int32)[None, :] + col_start
    mixing = (group_id * in_width + row_index) * width + col_index
    mixing = jnp.bitwise_xor(mixing, seed_step[0])
    mixing = mixing * 668265261 + seed_step[1] * 374761393
    mixing = jnp.bitwise_xor(mixing, jnp.right_shift(mixing, 15) & 131071)
    mixing = mixing * 739982445
    mixing = jnp.bitwise_xor(mixing, jnp.right_shift(mixing, 12) & 1048575)
    mixing = mixing * 695872825
    mixing = jnp.bitwise_xor(mixing, jnp.right_shift(mixing, 15) & 131071)
    first_unif = ((mixing & 4095).astype(jnp.float32) + 0.5) / 4096.0
    second_unif = ((jnp.right_shift(mixing, 12) & 4095).astype(jnp.float32) + 0.5) / 4096.0
    return 2.449489742783178 * (first_unif + second_unif - 1.0)


def ivon_update(mean, hess, momentum, grad_sum, curv_sum, groups):
    grad_mean = grad_sum / groups
    hess_est = curv_sum / groups
    new_momentum = decay_first * momentum + (1.0 - decay_first) * grad_mean
    new_hess = (
        decay_second * hess
        + (1.0 - decay_second) * hess_est
        + 0.5 * (1.0 - decay_second) ** 2 * (hess - hess_est) ** 2 / (hess + damping)
    )
    new_mean = mean - step_size * (new_momentum + damping * mean) / (new_hess + damping)
    return (new_mean, new_hess, new_momentum)


def row_major(value):
    return with_layout_constraint(value, Layout(major_to_minor=(0, 1)))


CHUNKS = 4


def per_device(seed_step, attn, resid, cotangent, gain, mean, hess, momentum):
    own_rows = mean.shape[0]
    width = mean.shape[1]
    in_width = attn.shape[1]
    scaling = in_width ** (-0.5)
    groups = lax.axis_size("sample")
    group_id = lax.axis_index("sample")
    shard_id = lax.axis_index("fsdp")
    part = width // CHUNKS
    cuts = [slice(c * part, (c + 1) * part) for c in range(CHUNKS)]
    epsilons, gathered = [], []
    for c, cut in enumerate(cuts):
        sigma = 1.0 / jnp.sqrt(ess_value * (hess[:, cut] + damping))
        epsilon = noise_table(
            seed_step, group_id, shard_id * own_rows, own_rows, in_width, width, c * part, part
        )
        sampled = (
            mean[:, cut].astype(jnp.bfloat16).astype(jnp.float32)
            + sigma.astype(jnp.bfloat16).astype(jnp.float32) * epsilon
        ).astype(jnp.bfloat16)
        epsilons.append(epsilon / sigma)
        gathered.append(lax.all_gather(row_major(sampled), "fsdp", axis=0, tiled=True))
    totals = []
    square = jnp.zeros((attn.shape[0], 1), jnp.float32)
    cross = jnp.zeros((attn.shape[0], 1), jnp.float32)
    for c, cut in enumerate(cuts):
        product = row_major(
            jnp.dot(attn, row_major(gathered[c]), preferred_element_type=jnp.float32)
        )
        total = resid[:, cut].astype(jnp.float32) + product * scaling
        upstream = gain[cut].astype(jnp.float32)[None, :] * cotangent[:, cut].astype(jnp.float32)
        square = square + jnp.sum(total * total, axis=-1, keepdims=True)
        cross = cross + jnp.sum(total * upstream, axis=-1, keepdims=True)
        totals.append(total)
    inverse = lax.rsqrt(square / width + norm_eps)
    slope = inverse**3 * (cross / width)
    sums = []
    for c, cut in enumerate(cuts):
        upstream = gain[cut].astype(jnp.float32)[None, :] * cotangent[:, cut].astype(jnp.float32)
        back_low = (inverse * upstream - totals[c] * slope).astype(jnp.bfloat16)
        grad = lax.psum_scatter(
            row_major(
                (
                    lax.dot_general(
                        attn,
                        row_major(back_low),
                        (((0,), (0,)), ((), ())),
                        preferred_element_type=jnp.float32,
                    )
                    * scaling
                ).astype(jnp.bfloat16)
            ),
            "fsdp",
            scatter_dimension=0,
            tiled=True,
        )
        if sums:
            grad, sums[-1] = lax.optimization_barrier((grad, sums[-1]))
        grad = row_major(grad)
        curvature = (grad.astype(jnp.float32) * epsilons[c]).astype(jnp.bfloat16)
        sums.append(lax.psum((grad, row_major(curvature)), "sample"))
    grad_sum = jnp.concatenate([s[0] for s in sums], axis=1).astype(jnp.float32)
    curv_sum = jnp.concatenate([s[1] for s in sums], axis=1).astype(jnp.float32)
    return ivon_update(mean, hess, momentum, grad_sum, curv_sum, groups)


def solution(mesh):
    placed = (
        P(),
        P(("sample", "fsdp"), None),
        P(("sample", "fsdp"), None),
        P(("sample", "fsdp"), None),
        P(),
        P("fsdp", None),
        P("fsdp", None),
        P("fsdp", None),
    )
    return jax.shard_map(
        per_device,
        mesh=mesh,
        in_specs=placed,
        out_specs=(P("fsdp", None), P("fsdp", None), P("fsdp", None)),
        check_vma=False,
    )
```

time: 531 us -> 672 us (1.27)
  waiting for transfers between devices: 405 us -> 563 us
  local copies, waits for them, and re-layouts: 48.1 us -> 1.41 us
  matrix products: 35.5 us -> 53.4 us
  other arithmetic: 26.6 us -> 37.2 us
    psum x1 -> x4, waiting for transfers between devices: 97.1 us -> 215 us  [per_device(): sums.append(lax.psum((grad, row_major(curvature)), 'sample'))]
    unnamed x14 -> x10, local copies, waits for them, and re-layouts: 46.7 us -> 0.02 us
    all_gather x1 -> x4, waiting for transfers between devices: 141 us -> 172 us  [per_device(): lax.all_gather(row_major(sampled), 'fsdp', axis=0, tiled=True)]
    dot_general x2 -> x8, matrix products: 35.5 us -> 53.4 us  [the longest x4 28.2 us: per_device(): jnp.dot(attn, row_major(gathered[c]), preferred_element_type=jnp.float32)]
    reduce_scatter x1 -> x4, waiting for transfers between devices: 166 us -> 174 us  [per_device(): lax.psum_scatter(row_major((lax.dot_general(attn, row_major(back_low), ((...]
    convert_element_type x3 -> x6, other arithmetic: 15.7 us -> 23 us  [the longest x4 15.5 us: per_device(): curvature = (grad.astype(jnp.float32) * epsilons[c]).astype(jnp.bfloat16)]
  transfers between devices with their start and end apart: 3 -> 12, of which waited for: 3 -> 12; matrix products, arithmetic and copies ran while one was open for 4% -> 7% of each run, Pallas kernels for 0% -> 0%
where the time goes in v1:
time: 672 us; the launch traced here: 671 us
  waiting for transfers between devices  563 us (84%)
  matrix products  53.4 us (8%)
  other arithmetic  37.2 us (6%)
  between operations  14.9 us (2%)
    psum x4, waiting for transfers between devices, per_device(): sums.append(lax.psum((grad, row_major(curvature)), 'sample'))  215 us
    reduce_scatter x4, waiting for transfers between devices, per_device(): lax.psum_scatter(row_major((lax.dot_general(attn, row_major(back_low), ((...  174 us
    all_gather x4, waiting for transfers between devices, per_device(): lax.all_gather(row_major(sampled), 'fsdp', axis=0, tiled=True)  172 us
    dot_general x4, matrix products, per_device(): jnp.dot(attn, row_major(gathered[c]), preferred_element_type=jnp.float32)  28.2 us
    dot_general x4, matrix products, per_device(): lax.dot_general(attn, row_major(back_low), (((0,), (0,)), ((), ())), pref...  25.2 us
    convert_element_type x4, other arithmetic, per_device(): curvature = (grad.astype(jnp.float32) * epsilons[c]).astype(jnp.bfloat16)  15.5 us
  transfers between devices with their start and end apart: 12, of which 12 were waited for; matrix products, arithmetic and copies ran while one was open for 7% of the time, Pallas kernels for 0%

profile of v1, /device:TPU:0, one launch (start us, length us, event | category | flops | bytes accessed | tf_op | source)
XLA Modules:
  0.0 671.1 jit_solution(17493066383043819291)
XLA Ops:
  7.3 1.4 fusion.36
  8.6 3.8 convert.6
  13.1 7.5 %add_convert_fusion.1 = (bf16[256,1024]{1,0:T(8,128)(2,1)}, bf16[256,1024]{1,0:T(8,128)(2,1)}, bf16[256,1024]{1,0:T(8,128)(2,1)}, bf16[256,1024]{1,0:T(8,128)(2,1)}) fusion(f32[256,4096]{1,0:T(8,128)} %param.14, bf16[256,4096]{1,0:T(8,128)(2,1)} %convert.6, s32[]{:T(128)} %bitcast.1, s32[]{:T(128)} %bitcast, s32[1024]{0:T(1024)S(1)} %get-tuple-element.54, ...), kind=kLoop, calls=%fused_computation.61 | loop fusion | flops 35651584 | bytes 8401928 | tf_op jit(solution)/shard_map/convert_element_type | solution.py:70
  20.7 0.7 all-gather.5.cloned.1.call-update
  21.4 0.7 all-gather.11.cloned.1.call-update
  22.2 0.5 all-gather.7.cloned.1.call-update
  22.9 47.7 %all-gather.9.cloned.1.call-done = bf16[2048,1024]{1,0:T(8,128)(2,1)} async-done(((bf16[256,1024]{1,0:T(8,128)(2,1)}), bf16[2048,1024]{1,0:T(8,128)(2,1)}) %all-gather.9.cloned.1.call-update) | async-done | bytes 4194320 | tf_op jit(solution)/shard_map/all_gather | solution.py:72
  70.6 6.2 fusion.11
  76.8 41.9 %all-gather.5.cloned.1.call-done = bf16[2048,1024]{1,0:T(8,128)(2,1)} async-done(((bf16[256,1024]{1,0:T(8,128)(2,1)}), bf16[2048,1024]{1,0:T(8,128)(2,1)}) %all-gather.5.cloned.1.call-update) | async-done | bytes 4194320 | tf_op jit(solution)/shard_map/all_gather | solution.py:72
  118.7 6.1 fusion.13
  124.8 41.4 %all-gather.11.cloned.1.call-done = bf16[2048,1024]{1,0:T(8,128)(2,1)} async-done(((bf16[256,1024]{1,0:T(8,128)(2,1)}), bf16[2048,1024]{1,0:T(8,128)(2,1)}) %all-gather.11.cloned.1.call-update) | async-done | bytes 4194320 | tf_op jit(solution)/shard_map/all_gather | solution.py:72
  166.2 6.1 fusion.10
  172.3 41.2 %all-gather.7.cloned.1.call-done = bf16[2048,1024]{1,0:T(8,128)(2,1)} async-done(((bf16[256,1024]{1,0:T(8,128)(2,1)}), bf16[2048,1024]{1,0:T(8,128)(2,1)}) %all-gather.7.cloned.1.call-update) | async-done | bytes 4194320 | tf_op jit(solution)/shard_map/all_gather | solution.py:72
  213.6 9.8 %multiply_reduce_fusion.2 = (f32[512]{0:T(512)S(1)}, f32[512]{0:T(512)S(1)}, f32[512]{0:T(512)S(1)}, f32[512]{0:T(512)S(1)}, f32[512]{0:T(512)S(1)}, /*index=5*/...) fusion(f32[1024]{0:T(1024)S(1)} %get-tuple-element.48, bf16[512,4096]{1,0:T(8,128)(2,1)} %param.11, ...), kind=kOutput, calls=%fused_computation.34 | convolution fusion | flops 2161635328 | bytes 19955712 | tf_op jit(solution)/shard_map/dot_general | solution.py:78
  223.4 5.9 fusion.7
  229.6 6.4 fusion.6
  236.1 42.1 %reduce-scatter.7.cloned.1.call-done = bf16[256,1024]{1,0:T(8,128)(2,1)} async-done(((bf16[2048,1024]{1,0:T(8,128)(2,1)}), bf16[256,1024]{1,0:T(8,128)(2,1)}) %reduce-scatter.7.cloned.1.call-update) | async-done | bytes 524304 | tf_op jit(solution)/shard_map/reduce_scatter | solution.py:91
  278.2 3.9 multiply_convert_fusion.7
  282.2 6.4 fusion.8
  288.7 40.4 %reduce-scatter.5.cloned.1.call-done = bf16[256,1024]{1,0:T(8,128)(2,1)} async-done(((bf16[2048,1024]{1,0:T(8,128)(2,1)}), bf16[256,1024]{1,0:T(8,128)(2,1)}) %reduce-scatter.5.cloned.1.call-update) | async-done | bytes 524304 | tf_op jit(solution)/shard_map/reduce_scatter | solution.py:91
  329.1 53.9 %all-reduce.15.cloned.1.call-done = (bf16[256,1024]{1,0:T(8,128)(2,1)}, bf16[256,1024]{1,0:T(8,128)(2,1)}) async-done(((bf16[256,1024]{1,0:T(8,128)(2,1)}, bf16[256,1024]{1,0:T(8,128)(2,1)}), (bf16[256,1024]{1,0:T(8,128)(2,1)}, bf16[256,1024]{1,0:T(8,128)(2,1)})) %all-reduce.15.cloned.1.call-update) | async-done | bytes 1048592 | tf_op jit(solution)/shard_map/psum | solution.py:111
  383.0 3.9 multiply_convert_fusion.6
  386.9 6.4 fusion.9
  393.5 42.5 %reduce-scatter.9.cloned.1.call-done = bf16[256,1024]{1,0:T(8,128)(2,1)} async-done(((bf16[2048,1024]{1,0:T(8,128)(2,1)}), bf16[256,1024]{1,0:T(8,128)(2,1)}) %reduce-scatter.9.cloned.1.call-update) | async-done | bytes 524304 | tf_op jit(solution)/shard_map/reduce_scatter | solution.py:91
  435.9 53.9 %all-reduce.13.cloned.1.call-done = (bf16[256,1024]{1,0:T(8,128)(2,1)}, bf16[256,1024]{1,0:T(8,128)(2,1)}) async-done(((bf16[256,1024]{1,0:T(8,128)(2,1)}, bf16[256,1024]{1,0:T(8,128)(2,1)}), (bf16[256,1024]{1,0:T(8,128)(2,1)}, bf16[256,1024]{1,0:T(8,128)(2,1)})) %all-reduce.13.cloned.1.call-update) | async-done | bytes 1048592 | tf_op jit(solution)/shard_map/psum | solution.py:111
  489.9 3.9 multiply_convert_fusion.5
  493.8 0.3 all-reduce.9.cloned.1.call-start
  494.1 48.6 %reduce-scatter.11.cloned.1.call-done = bf16[256,1024]{1,0:T(8,128)(2,1)} async-done(((bf16[2048,1024]{1,0:T(8,128)(2,1)}), bf16[256,1024]{1,0:T(8,128)(2,1)}) %reduce-scatter.11.cloned.1.call-update) | async-done | bytes 524304 | tf_op jit(solution)/shard_map/reduce_scatter | solution.py:91
  542.6 54.5 %all-reduce.11.cloned.1.call-done = (bf16[256,1024]{1,0:T(8,128)(2,1)}, bf16[256,1024]{1,0:T(8,128)(2,1)}) async-done(((bf16[256,1024]{1,0:T(8,128)(2,1)}, bf16[256,1024]{1,0:T(8,128)(2,1)}), (bf16[256,1024]{1,0:T(8,128)(2,1)}, bf16[256,1024]{1,0:T(8,128)(2,1)})) %all-reduce.11.cloned.1.call-update) | async-done | bytes 1048592 | tf_op jit(solution)/shard_map/psum | solution.py:111
  597.2 3.9 multiply_convert_fusion.4
  601.0 52.9 %all-reduce.9.cloned.1.call-done = (bf16[256,1024]{1,0:T(8,128)(2,1)}, bf16[256,1024]{1,0:T(8,128)(2,1)}) async-done(((bf16[256,1024]{1,0:T(8,128)(2,1)}, bf16[256,1024]{1,0:T(8,128)(2,1)}), (bf16[256,1024]{1,0:T(8,128)(2,1)}, bf16[256,1024]{1,0:T(8,128)(2,1)})) %all-reduce.9.cloned.1.call-update) | async-done | bytes 1048592 | tf_op jit(solution)/shard_map/psum | solution.py:111
  653.9 10.4 %divide_subtract_fusion = (f32[256,4096]{1,0:T(8,128)}, f32[256,4096]{1,0:T(8,128)}, f32[256,4096]{1,0:T(8,128)}) fusion(f32[256,4096]{1,0:T(8,128)} %param.13, bf16[256,1024]{1,0:T(8,128)(2,1)} %get-tuple-element.30, bf16[256,1024]{1,0:T(8,128)(2,1)} %get-tuple-element.16, bf16[256,1024]{1,0:T(8,128)(2,1)} %get-tuple-element.14, ...), kind=kLoop, calls=%fused_computation.12 | loop fusion | flops 36700160 | bytes 29360128 | tf_op jit(solution)/shard_map/sub | solution.py:40
  (35 shorter events, 1.1 us)
Async XLA Ops:
  7.2 63.5 %copy-start = (bf16[512,2048]{1,0:T(8,128)(2,1)S(1)}, bf16[512,2048]{1,0:T(8,128)(2,1)}, u32[]{:S(2)}) copy-start(bf16[512,2048]{1,0:T(8,128)(2,1)} %param.9) | copy-start | bytes 6291460
  7.2 63.4 %all-gather.9.cloned.1.call-start = ((), (), s32[]{:S(2)}) async-start(), calls=%async_computation.6 | async-start | bytes 4718592 | tf_op jit(solution)/shard_map/all_gather | solution.py:72
  20.6 2.3 copy-start.3
  20.6 98.1 %all-gather.5.cloned.1.call-start = ((), (), s32[]{:S(2)}) async-start(), calls=%async_computation.4 | async-start | bytes 4718592 | tf_op jit(solution)/shard_map/all_gather | solution.py:72
  21.4 144.8 %all-gather.11.cloned.1.call-start = ((), (), s32[]{:S(2)}) async-start(), calls=%async_computation.7 | async-start | bytes 4718592 | tf_op jit(solution)/shard_map/all_gather | solution.py:72
  22.1 191.4 %all-gather.7.cloned.1.call-start = ((), (), s32[]{:S(2)}) async-start(), calls=%async_computation.5 | async-start | bytes 4718592 | tf_op jit(solution)/shard_map/all_gather | solution.py:72
  22.7 255.5 %reduce-scatter.7.cloned.1.call-start = ((), (), s32[]{:S(2)}) async-start(), calls=%async_computation.9 | async-start | bytes 4718592 | tf_op jit(solution)/shard_map/reduce_scatter | solution.py:91
  213.6 9.8 %copy-start.4 = (f32[512,1024]{1,0:T(8,128)S(1)}, f32[512,1024]{1,0:T(8,128)}, u32[]{:S(2)}) copy-start(f32[512,1024]{1,0:T(8,128)} %fusion.13) | copy-start | bytes 6291460
  229.3 99.8 %reduce-scatter.5.cloned.1.call-start = ((), (), s32[]{:S(2)}) async-start(), calls=%async_computation.8 | async-start | bytes 4718592 | tf_op jit(solution)/shard_map/reduce_scatter | solution.py:91
  236.0 147.0 %all-reduce.15.cloned.1.call-start = ((), (), s32[]{:S(2)}) async-start(), calls=%async_computation.15 | async-start | bytes 2097152 | tf_op jit(solution)/shard_map/psum | solution.py:111
  282.1 153.8 %reduce-scatter.9.cloned.1.call-start = ((), (), s32[]{:S(2)}) async-start(), calls=%async_computation.10 | async-start | bytes 4718592 | tf_op jit(solution)/shard_map/reduce_scatter | solution.py:91
  288.6 201.3 %all-reduce.13.cloned.1.call-start = ((), (), s32[]{:S(2)}) async-start(), calls=%async_computation.14 | async-start | bytes 2097152 | tf_op jit(solution)/shard_map/psum | solution.py:111
  386.9 155.7 %reduce-scatter.11.cloned.1.call-start = ((), (), s32[]{:S(2)}) async-start(), calls=%async_computation.11 | async-start | bytes 4718592 | tf_op jit(solution)/shard_map/reduce_scatter | solution.py:91
  393.4 203.7 %all-reduce.11.cloned.1.call-start = ((), (), s32[]{:S(2)}) async-start(), calls=%async_computation.13 | async-start | bytes 2097152 | tf_op jit(solution)/shard_map/psum | solution.py:111
  493.7 160.2 %copy-start.1 = (bf16[256,1024]{1,0:T(8,128)(2,1)S(1)}, bf16[256,1024]{1,0:T(8,128)(2,1)}, u32[]{:S(2)}) copy-start(bf16[256,1024]{1,0:T(8,128)(2,1)} %get-tuple-element.12) | copy-start | bytes 1572868
  493.7 160.2 %copy-start.2 = (bf16[256,1024]{1,0:T(8,128)(2,1)S(1)}, bf16[256,1024]{1,0:T(8,128)(2,1)}, u32[]{:S(2)}) copy-start(bf16[256,1024]{1,0:T(8,128)(2,1)} %get-tuple-element.18) | copy-start | bytes 1572868
  493.8 160.2 %all-reduce.9.cloned.1.call-start = ((), (), s32[]{:S(2)}) async-start(), calls=%async_computation.12 | async-start | bytes 2097152 | tf_op jit(solution)/shard_map/psum | solution.py:111
Sparse Core Ops, SparseCore 0:
  20.7 49.8 all-gather.8
  72.8 45.8 all-gather.4
  120.3 45.8 all-gather.10
  167.7 45.8 all-gather.6
  229.4 48.7 reduce-scatter.6
  280.9 48.1 reduce-scatter.4
  332.1 50.8 all-reduce.14
  385.9 50.0 reduce-scatter.8
  439.0 50.8 all-reduce.12
  492.6 50.0 reduce-scatter.10
  546.3 50.8 all-reduce.10
  601.1 52.7 all-reduce.8

commit v2 on v0

--- a/solution.py
+++ b/solution.py
@@ -1,6 +1,10 @@
+import functools
+
 import jax
 import jax.numpy as jnp
 from jax import lax
+from jax.experimental import pallas as pl
+from jax.experimental.pallas import tpu as pltpu
 from jax.sharding import PartitionSpec as P
 
 ess_value = 10.0
@@ -40,6 +44,373 @@
     return (new_mean, new_hess, new_momentum)
 
 
+MESH = pl.DeviceIdType.MESH
+PIECES = 4
+
+
+def exchange_kernel(
+    line, groups, scaling,
+    attn, attn_t, gain, sampled, resid, cotangent, out,
+    weights, back, total, paired, chained, ready,
+    local_sem, weight_recv, up_send, down_send, core_send,
+    pair_send, pair_recv, chain_send, chain_recv, group_send, group_recv,
+):
+    group = lax.axis_index("sample")
+    shard = lax.axis_index("fsdp")
+    place = lax.div(shard, 2)
+    core = lax.rem(shard, 2)
+    twin = place * 2 + 1 - core
+    rows, width = sampled.shape
+    tokens = attn.shape[0]
+    part = width // PIECES
+    last = line - 1
+
+    take_resid = pltpu.make_async_copy(resid, back, local_sem.at[0])
+    take_resid.start()
+    take_own = pltpu.make_async_copy(sampled, weights.at[shard], local_sem.at[1])
+    take_own.start()
+
+    barrier = pltpu.get_barrier_semaphore()
+    above = lax.rem(place + 1, line) * 2 + core
+    below = lax.rem(place + last, line) * 2 + core
+    for other in (twin, above, below):
+        pl.semaphore_signal(barrier, inc=1, device_id={"fsdp": other}, device_id_type=MESH)
+    for step in range(1, groups):
+        pl.semaphore_signal(
+            barrier, inc=1, device_id={"sample": lax.rem(group + step, groups)}, device_id_type=MESH
+        )
+    pl.semaphore_wait(barrier, groups + 2)
+    take_own.wait()
+
+    def weight_copy(slot, send, other):
+        return pltpu.make_async_remote_copy(
+            src_ref=weights.at[slot],
+            dst_ref=weights.at[slot],
+            send_sem=send,
+            recv_sem=weight_recv.at[slot],
+            device_id={"fsdp": other},
+            device_id_type=MESH,
+        )
+
+    def wait_weight(slot):
+        weight_copy(slot, core_send.at[0], twin).wait_recv()
+
+    def pass_on(slot, up, down):
+        if up is not None:
+            @pl.when(place < last)
+            def _():
+                weight_copy(slot, up_send.at[up], above).start()
+        if down is not None:
+            @pl.when(place > 0)
+            def _():
+                weight_copy(slot, down_send.at[down], below).start()
+        weight_copy(slot, core_send.at[lax.div(slot, 2)], twin).start()
+
+    pass_on(shard, 0, 0)
+
+    take_resid.wait()
+
+    def widen(r, carry):
+        sl = pl.ds(pl.multiple_of(r * 32, 32), 32)
+        total[sl, :] = back[sl, :].astype(jnp.float32) * (1.0 / scaling)
+        return carry
+
+    lax.fori_loop(0, tokens // 32, widen, 0)
+    take_cot = pltpu.make_async_copy(cotangent, back, local_sem.at[0])
+    take_cot.start()
+
+    def multiply(slot):
+        lhs = attn[:, pl.ds(pl.multiple_of(slot * rows, rows), rows)]
+
+        def columns(j, carry):
+            sl = pl.ds(pl.multiple_of(j * 512, 512), 512)
+            total[:, sl] += jnp.dot(lhs, weights[slot, :, sl], preferred_element_type=jnp.float32)
+            return carry
+
+        lax.fori_loop(0, width // 512, columns, 0)
+
+    def multiply_all(slots):
+        def one(i, carry):
+            slot = slots[-1][0]
+            for k in range(len(slots) - 1):
+                slot = jnp.where(i == k, slots[k][0], slot)
+            wanted = slots[-1][1]
+            for k in range(len(slots) - 1):
+                wanted = jnp.where(i == k, slots[k][1], wanted)
+            from_twin = lax.rem(slot, 2) != core
+
+            @pl.when(wanted)
+            def _():
+                @pl.when(from_twin)
+                def _():
+                    wait_weight(slot)
+                multiply(slot)
+            return carry
+
+        lax.fori_loop(0, len(slots), one, 0)
+
+    always = place >= 0
+    multiply_all([(shard, always), (twin, always)])
+
+    def gather_step(t, carry):
+        low = place - 1 - t
+        high = place + 1 + t
+        low_slot = jnp.maximum(low, 0) * 2 + core
+        high_slot = jnp.minimum(high, last) * 2 + core
+
+        @pl.when(low >= 0)
+        def _():
+            wait_weight(low_slot)
+            pass_on(low_slot, t + 1, None)
+
+        @pl.when(high <= last)
+        def _():
+            wait_weight(high_slot)
+            pass_on(high_slot, None, t + 1)
+
+        multiply_all([
+            (low_slot, low >= 0),
+            (high_slot, high <= last),
+            (low_slot + 1 - 2 * core, low >= 0),
+            (high_slot + 1 - 2 * core, high <= last),
+        ])
+        return carry
+
+    lax.fori_loop(0, last, gather_step, 0)
+
+    def drain_weights(t, carry):
+        @pl.when((place < last) & (place - t >= 0))
+        def _():
+            weight_copy(shard, up_send.at[t], above).wait_send()
+
+        @pl.when((place > 0) & (place + t <= last))
+        def _():
+            weight_copy(shard, down_send.at[t], below).wait_send()
+
+        weight_copy(shard, core_send.at[t], twin).wait_send()
+        return carry
+
+    lax.fori_loop(0, line, drain_weights, 0)
+
+    take_cot.wait()
+    span = 512
+
+    def normalise(r, carry):
+        sl = pl.ds(pl.multiple_of(r * 16, 16), 16)
+        square = jnp.zeros((16, span), jnp.float32)
+        cross = jnp.zeros((16, span), jnp.float32)
+        for c in range(width // span):
+            cs = pl.ds(c * span, span)
+            value = total[sl, cs] * scaling
+            upstream = gain[:, cs] * back[sl, cs].astype(jnp.float32)
+            square = square + value * value
+            cross = cross + value * upstream
+        inverse = lax.rsqrt(jnp.sum(square, axis=-1, keepdims=True) * (1.0 / width) + norm_eps)
+        slope = inverse * inverse * inverse * (
+            jnp.sum(cross, axis=-1, keepdims=True) * (1.0 / width)
+        )
+        for c in range(width // span):
+            cs = pl.ds(c * span, span)
+            value = total[sl, cs] * scaling
+            upstream = gain[:, cs] * back[sl, cs].astype(jnp.float32)
+            back[sl, cs] = (inverse * upstream - value * slope).astype(jnp.bfloat16)
+        return carry
+
+    lax.fori_loop(0, tokens // 16, normalise, 0)
+
+    def partial(block, piece):
+        lhs = attn_t[pl.ds(pl.multiple_of(block * rows, rows), rows), :]
+        rhs = back[:, pl.ds(pl.multiple_of(piece * part, part), part)]
+        return jnp.dot(lhs, rhs, preferred_element_type=jnp.float32) * scaling
+
+    def pair_copy(goal, piece):
+        return pltpu.make_async_remote_copy(
+            src_ref=weights.at[goal, :, pl.ds(pl.multiple_of(piece * part, part), part)],
+            dst_ref=paired.at[goal, piece],
+            send_sem=pair_send.at[goal, piece],
+            recv_sem=pair_recv.at[goal, piece],
+            device_id={"fsdp": twin},
+            device_id_type=MESH,
+        )
+
+    def give_twin(i, piece):
+        goal = i
+        weights[goal, :, pl.ds(pl.multiple_of(piece * part, part), part)] = partial(
+            goal * 2 + 1 - core, piece
+        ).astype(jnp.bfloat16)
+        pair_copy(goal, piece).start()
+        return piece
+
+    def chain_copy(goal, slot, piece, other):
+        return pltpu.make_async_remote_copy(
+            src_ref=chained.at[goal, piece],
+            dst_ref=chained.at[slot, piece],
+            send_sem=chain_send.at[goal, piece],
+            recv_sem=chain_recv.at[slot, piece],
+            device_id={"fsdp": other},
+            device_id_type=MESH,
+        )
+
+    def own_term(goal, piece):
+        pair_copy(goal, piece).wait_recv()
+        return partial(goal * 2 + core, piece) + paired[goal, piece].astype(jnp.float32)
+
+    def forward(goal, piece, first, slot, other):
+        @pl.when(first)
+        def _():
+            chained[goal, piece] = own_term(goal, piece).astype(jnp.bfloat16)
+
+        @pl.when(jnp.logical_not(first))
+        def _():
+            chain_copy(goal, goal, piece, other).wait_recv()
+            chained[goal, piece] = (
+                own_term(goal, piece) + chained[goal, piece].astype(jnp.float32)
+            ).astype(jnp.bfloat16)
+
+        chain_copy(goal, slot, piece, other).start()
+
+    def group_copy(piece, step):
+        cs = pl.ds(pl.multiple_of(piece * part, part), part)
+        return pltpu.make_async_remote_copy(
+            src_ref=ready.at[piece],
+            dst_ref=out.at[group, :, cs],
+            send_sem=group_send.at[step, piece],
+            recv_sem=group_recv.at[group, piece],
+            device_id={"sample": lax.rem(group + step, groups)},
+            device_id_type=MESH,
+        )
+
+    def keep_copy(piece):
+        cs = pl.ds(pl.multiple_of(piece * part, part), part)
+        return pltpu.make_async_copy(
+            ready.at[piece], out.at[group, :, cs], group_send.at[0, piece]
+        )
+
+    @pl.when(place == 0)
+    def _():
+        chained[0] = jnp.zeros(chained.shape[1:], chained.dtype)
+
+    @pl.when(place == last)
+    def _():
+        chained[line] = jnp.zeros(chained.shape[1:], chained.dtype)
+
+    lax.fori_loop(0, line, give_twin, 0)
+
+    def reduce_step(step, carry):
+        up_at = step - place
+        up_piece = lax.div(jnp.maximum(up_at, 0), last)
+        up_goal = last - lax.rem(jnp.maximum(up_at, 0), last)
+
+        @pl.when((up_at >= 0) & (up_piece < PIECES) & (up_goal > place))
+        def _():
+            forward(up_goal, up_piece, place == 0, up_goal, above)
+
+        down_at = step - (last - place)
+        down_piece = lax.div(jnp.maximum(down_at, 0), last)
+        down_goal = lax.rem(jnp.maximum(down_at, 0), last)
+
+        @pl.when((down_at >= 0) & (down_piece < PIECES) & (down_goal < place))
+        def _():
+            slot = jnp.where(down_goal == place - 1, line, down_goal)
+            forward(down_goal, down_piece, place == last, slot, below)
+
+        turn = lax.div(step, last)
+
+        @pl.when((lax.rem(step, last) == 0) & (turn < PIECES - 1))
+        def _():
+            lax.fori_loop(0, line, give_twin, turn + 1)
+
+        @pl.when((lax.rem(step, last) == 0) & (turn >= 1))
+        def _():
+            piece = turn - 1
+
+            @pl.when(place > 0)
+            def _():
+                chain_copy(place, place, piece, below).wait_recv()
+
+            @pl.when(place < last)
+            def _():
+                chain_copy(place, line, piece, above).wait_recv()
+
+            ready[piece] = (
+                own_term(place, piece)
+                + chained[place, piece].astype(jnp.float32)
+                + chained[line, piece].astype(jnp.float32)
+            ).astype(jnp.bfloat16)
+            for k in range(1, groups):
+                group_copy(piece, k).start()
+            keep_copy(piece).start()
+        return carry
+
+    lax.fori_loop(0, PIECES * last + 1, reduce_step, 0)
+
+    def finish(piece, carry):
+        def goals(goal, inner):
+            pair_copy(goal, piece).wait_send()
+
+            @pl.when(goal != place)
+            def _():
+                chain_copy(goal, goal, piece, above).wait_send()
+            return inner
+
+        lax.fori_loop(0, line, goals, 0)
+        keep_copy(piece).wait()
+        for k in range(1, groups):
+            group_copy(piece, k).wait_send()
+            source = lax.rem(group + k, groups)
+            cs = pl.ds(pl.multiple_of(piece * part, part), part)
+            pltpu.make_async_remote_copy(
+                src_ref=ready.at[piece],
+                dst_ref=out.at[source, :, cs],
+                send_sem=group_send.at[k, piece],
+                recv_sem=group_recv.at[source, piece],
+                device_id={"sample": source},
+                device_id_type=MESH,
+            ).wait_recv()
+        return carry
+
+    lax.fori_loop(0, PIECES, finish, 0)
+
+
+def exchange(attn, resid, cotangent, gain, sampled, scaling):
+    line = lax.axis_size("fsdp") // 2
+    groups = lax.axis_size("sample")
+    tokens, width = resid.shape
+    rows = sampled.shape[0]
+    part = width // PIECES
+    vmem = pl.BlockSpec(memory_space=pltpu.VMEM)
+    hbm = pl.BlockSpec(memory_space=pl.ANY)
+    dma = pltpu.SemaphoreType.DMA
+    return pl.pallas_call(
+        functools.partial(exchange_kernel, line, groups, scaling),
+        out_shape=jax.ShapeDtypeStruct((groups, rows, width), jnp.bfloat16),
+        in_specs=[vmem, vmem, vmem, hbm, hbm, hbm],
+        out_specs=hbm,
+        scratch_shapes=[
+            pltpu.VMEM((2 * line, rows, width), jnp.bfloat16),
+            pltpu.VMEM((tokens, width), jnp.bfloat16),
+            pltpu.VMEM((tokens, width), jnp.float32),
+            pltpu.VMEM((line, PIECES, rows, part), jnp.bfloat16),
+            pltpu.VMEM((line + 1, PIECES, rows, part), jnp.bfloat16),
+            pltpu.VMEM((PIECES, rows, part), jnp.bfloat16),
+            dma((2,)),
+            dma((2 * line,)),
+            dma((line,)),
+            dma((line,)),
+            dma((line,)),
+            dma((line, PIECES)),
+            dma((line, PIECES)),
+            dma((line, PIECES)),
+            dma((line + 1, PIECES)),
+            dma((groups, PIECES)),
+            dma((groups, PIECES)),
+        ],
+        compiler_params=pltpu.CompilerParams(
+            collective_id=0, has_side_effects=True, vmem_limit_bytes=60 * 2**20
+        ),
+    )(attn, attn.T, gain.astype(jnp.float32)[None, :], sampled, resid, cotangent)
+
+
 def per_device(seed_step, attn, resid, cotangent, gain, mean, hess, momentum):
     own_rows = mean.shape[0]
     width = mean.shape[1]
@@ -47,44 +418,22 @@
     scaling = in_width ** (-0.5)
     groups = lax.axis_size("sample")
     group_id = lax.axis_index("sample")
-    shard_id = lax.axis_index("fsdp")
+    row_start = lax.axis_index("fsdp") * own_rows
     sigma = 1.0 / jnp.sqrt(ess_value * (hess + damping))
-    epsilon = noise_table(seed_step, group_id, shard_id * own_rows, own_rows, in_width, width)
+    epsilon = noise_table(seed_step, group_id, row_start, own_rows, in_width, width)
     sampled = (
         mean.astype(jnp.bfloat16).astype(jnp.float32)
         + sigma.astype(jnp.bfloat16).astype(jnp.float32) * epsilon
     ).astype(jnp.bfloat16)
-    columns = attn
-    product = jnp.dot(
-        columns,
-        lax.all_gather(sampled, "fsdp", axis=0, tiled=True),
-        preferred_element_type=jnp.float32,
-    )
-    total = resid.astype(jnp.float32) + product * scaling
-    inverse = lax.rsqrt(jnp.mean(total * total, axis=-1, keepdims=True) + norm_eps)
-    upstream = gain.astype(jnp.float32)[None, :] * cotangent.astype(jnp.float32)
-    back = inverse * upstream - total * inverse**3 * jnp.mean(
-        total * upstream, axis=-1, keepdims=True
-    )
-    back_low = back.astype(jnp.bfloat16)
-    columns = attn
-    grad = lax.psum_scatter(
-        (
-            lax.dot_general(
-                columns, back_low, (((0,), (0,)), ((), ())), preferred_element_type=jnp.float32
-            )
-            * scaling
-        ).astype(jnp.bfloat16),
-        "fsdp",
-        scatter_dimension=0,
-        tiled=True,
-    ).astype(jnp.float32)
-    curvature = grad * epsilon / sigma
-    grad_sum, curv_sum = (
-        lax.psum(grad.astype(jnp.bfloat16), "sample").astype(jnp.float32),
-        lax.psum(curvature.astype(jnp.bfloat16), "sample").astype(jnp.float32),
-    )
-    return ivon_update(mean, hess, momentum, grad_sum, curv_sum, groups)
+    grads = exchange(attn, resid, cotangent, gain, sampled, scaling)
+    grad_sum = jnp.zeros((own_rows, width), jnp.float32)
+    curv_sum = jnp.zeros((own_rows, width), jnp.float32)
+    for g in range(groups):
+        grad = grads[g].astype(jnp.float32)
+        noise = noise_table(seed_step, g, row_start, own_rows, in_width, width)
+        grad_sum = grad_sum + grad
+        curv_sum = curv_sum + grad * noise
+    return ivon_update(mean, hess, momentum, grad_sum, curv_sum / sigma, groups)
 
 
 def solution(mesh):

time: 531 us -> 361 us (0.68)
  waiting for transfers between devices: 405 us -> 0 us
  Pallas kernels: 0 us -> 322 us
  local copies, waits for them, and re-layouts: 48.1 us -> 3.81 us
  matrix products: 35.5 us -> 0 us
  between operations: 14.4 us -> 1.32 us
  other arithmetic: 26.6 us -> 34.3 us
    pallas_call x0 -> x1, Pallas kernels: none -> 322 us  [exchange(): pl.pallas_call(functools.partial(exchange_kernel, line, groups, scaling),...]
    reduce_scatter x1 -> x0, waiting for transfers between devices: 166 us -> none  [per_device(): lax.psum_scatter((lax.dot_general(columns, back_low, (((0,), (0,)), ((),...]
    all_gather x1 -> x0, waiting for transfers between devices: 141 us -> none  [per_device(): lax.all_gather(sampled, 'fsdp', axis=0, tiled=True)]
    psum x1 -> x0, waiting for transfers between devices: 97.1 us -> none  [per_device(): lax.psum(curvature.astype(jnp.bfloat16), 'sample').astype(jnp.float32)]
    unnamed x14 -> x3, local copies, waits for them, and re-layouts: 46.7 us -> 2.49 us
    dot_general x2 -> x0, matrix products: 35.5 us -> none  [the longest x1 18.1 us: per_device(): lax.dot_general(columns, back_low, (((0,), (0,)), ((), ())), preferred_el...]
    sub x1, other arithmetic: 10.9 us -> 24.9 us  [ivon_update(): mean - step_size * (new_momentum + damping * mean) / (new_hess + damping)]
    convert_element_type x2 -> x0, other arithmetic: 7.85 us -> none  [the longest x1 7.85 us: per_device(): curvature.astype(jnp.bfloat16)]
  transfers between devices with their start and end apart: 3 -> 0, of which waited for: 3 -> 0; matrix products, arithmetic and copies ran while one was open for 4% -> 0% of each run, Pallas kernels for 0% -> 0%
where the time goes in v2:
time: 361 us
  Pallas kernels  322 us (89%)
  other arithmetic  34.3 us (10%)
  local copies, waits for them, and re-layouts  3.81 us (1%)
    pallas_call x1, Pallas kernels, exchange(): pl.pallas_call(functools.partial(exchange_kernel, line, groups, scaling),...  322 us
    sub x1, other arithmetic, ivon_update(): mean - step_size * (new_momentum + damping * mean) / (new_hess + damping)  24.9 us
    convert_element_type x1, other arithmetic, per_device(): sampled = (mean.astype(jnp.bfloat16).astype(jnp.float32) + sigma.astype(j...  8.04 us

profile of v2, /device:TPU:0, one launch (start us, length us, event | category | flops | bytes accessed | tf_op | source)
XLA Modules:
  0.0 361.0 jit_solution(14958148201866339535)
XLA Ops:
  0.6 1.3 fusion.9
  2.6 1.3 broadcast_in_dim.6
  3.9 0.0 copy-start
  3.9 8.0 %add_convert_fusion.sampled = bf16[256,4096]{1,0:T(8,128)(2,1)} fusion(f32[256,4096]{1,0:T(8,128)} %param.14, s32[]{:T(128)} %bitcast.3, s32[]{:T(128)} %bitcast.2, s32[256]{0:T(256)S(1)} %get-tuple-element.11, f32[256,4096]{1,0:T(8,128)} %param.13), kind=kLoop, calls=%fused_computation.15 | loop fusion | flops 36700160 | bytes 10486792 | tf_op jit(solution)/shard_map/convert_element_type | solution.py:427
  12.0 0.0 copy-done
  12.0 2.5 copy.11
  14.5 321.6 %shard_map.103 = bf16[4,256,4096]{2,1,0:T(8,128)(2,1)} custom-call(bf16[512,2048]{1,0:T(8,128)(2,1)} %attn.1, bf16[2048,512]{1,0:T(8,128)(2,1)} %bitcast.28, f32[1,4096]{1,0:T(1,128)} %bitcast.29, bf16[256,4096]{1,0:T(8,128)(2,1)} %add_convert_fusion.sampled, bf16[512,4096]{1,0:T(8,128)(2,1)} %resid.1, bf16[512,4096]{1,0:T(8,128)(2,1)} %cotangent.1), custom_call_target="tpu_custom_call" | custom-call | tf_op jit(solution)/shard_map/pallas_call | solution.py:384
  336.1 24.9 %divide_subtract_fusion = (f32[256,4096]{1,0:T(8,128)}, f32[256,4096]{1,0:T(8,128)}, f32[256,4096]{1,0:T(8,128)}) fusion(f32[256,4096]{1,0:T(8,128)} %param.13, bf16[4,256,4096]{2,1,0:T(8,128)(2,1)} %shard_map.103, f32[256,4096]{1,0:T(8,128)} %param.15, f32[256,4096]{1,0:T(8,128)} %param.14, s32[256]{0:T(256)S(1)} %get-tuple-element.8, ...), kind=kLoop, calls=%fused_computation.13 | loop fusion | flops 145752064 | bytes 33558536 | tf_op jit(solution)/shard_map/sub | solution.py:43
  (3 shorter events, 0.0 us)
Async XLA Ops:
  3.9 8.0 %copy-start = (bf16[512,2048]{1,0:T(8,128)(2,1)S(1)}, bf16[512,2048]{1,0:T(8,128)(2,1)}, u32[]{:S(2)}) copy-start(bf16[512,2048]{1,0:T(8,128)(2,1)} %attn.1) | copy-start | bytes 6291460

commit v3 on v2

--- a/solution.py
+++ b/solution.py
@@ -15,20 +15,26 @@
 norm_eps = 1e-05
 
 
-def noise_table(seed_step, group_id, row_start, row_count, in_width, width):
-    row_index = jnp.arange(row_count, dtype=jnp.int32)[:, None] + row_start
-    col_index = jnp.arange(width, dtype=jnp.int32)[None, :]
-    mixing = (group_id * in_width + row_index) * width + col_index
-    mixing = jnp.bitwise_xor(mixing, seed_step[0])
-    mixing = mixing * 668265261 + seed_step[1] * 374761393
+noise_scale = 2.449489742783178
+
+
+def noise_count(mixing, seed, key):
+    mixing = jnp.bitwise_xor(mixing, seed)
+    mixing = mixing * 668265261 + key
     mixing = jnp.bitwise_xor(mixing, jnp.right_shift(mixing, 15) & 131071)
     mixing = mixing * 739982445
     mixing = jnp.bitwise_xor(mixing, jnp.right_shift(mixing, 12) & 1048575)
     mixing = mixing * 695872825
     mixing = jnp.bitwise_xor(mixing, jnp.right_shift(mixing, 15) & 131071)
-    first_unif = ((mixing & 4095).astype(jnp.float32) + 0.5) / 4096.0
-    second_unif = ((jnp.right_shift(mixing, 12) & 4095).astype(jnp.float32) + 0.5) / 4096.0
-    return 2.449489742783178 * (first_unif + second_unif - 1.0)
+    return (mixing & 4095) + (jnp.right_shift(mixing, 12) & 4095)
+
+
+def noise_table(seed_step, group_id, row_start, row_count, in_width, width):
+    row_index = jnp.arange(row_count, dtype=jnp.int32)[:, None] + row_start
+    col_index = jnp.arange(width, dtype=jnp.int32)[None, :]
+    mixing = (group_id * in_width + row_index) * width + col_index
+    count = noise_count(mixing, seed_step[0], seed_step[1] * 374761393)
+    return noise_scale * ((count.astype(jnp.float32) + 1.0) / 4096.0 - 1.0)
 
 
 def ivon_update(mean, hess, momentum, grad_sum, curv_sum, groups):
@@ -45,14 +51,16 @@
 
 
 MESH = pl.DeviceIdType.MESH
-PIECES = 4
+PIECES = 8
+SLICES = 4
+SPAN = 512
 
 
 def exchange_kernel(
     line, groups, scaling,
-    attn, attn_t, gain, sampled, resid, cotangent, out,
-    weights, back, total, paired, chained, ready,
-    local_sem, weight_recv, up_send, down_send, core_send,
+    seed_step, attn, attn_t, gain, sampled, resid, cotangent, out, noise_out,
+    weights, back, total, paired, chained, ready, stage,
+    noise_sem, local_sem, weight_recv, up_send, down_send, core_send,
     pair_send, pair_recv, chain_send, chain_recv, group_send, group_recv,
 ):
     group = lax.axis_index("sample")
@@ -61,7 +69,7 @@
     core = lax.rem(shard, 2)
     twin = place * 2 + 1 - core
     rows, width = sampled.shape
-    tokens = attn.shape[0]
+    tokens, in_width = attn.shape
     part = width // PIECES
     last = line - 1
 
@@ -82,31 +90,76 @@
     pl.semaphore_wait(barrier, groups + 2)
     take_own.wait()
 
-    def weight_copy(slot, send, other):
+    piece_width = width // SLICES
+
+    def weight_copy(slot, h, send, other):
+        cs = pl.ds(pl.multiple_of(h * piece_width, piece_width), piece_width)
         return pltpu.make_async_remote_copy(
-            src_ref=weights.at[slot],
-            dst_ref=weights.at[slot],
+            src_ref=weights.at[slot, :, cs],
+            dst_ref=weights.at[slot, :, cs],
             send_sem=send,
-            recv_sem=weight_recv.at[slot],
+            recv_sem=weight_recv.at[slot, h],
             device_id={"fsdp": other},
             device_id_type=MESH,
         )
 
-    def wait_weight(slot):
-        weight_copy(slot, core_send.at[0], twin).wait_recv()
-
-    def pass_on(slot, up, down):
+    def wait_weight(slot, h):
+        weight_copy(slot, h, core_send.at[0, h], twin).wait_recv()
+
+    def pass_on(slot, h, up, down):
         if up is not None:
             @pl.when(place < last)
             def _():
-                weight_copy(slot, up_send.at[up], above).start()
+                weight_copy(slot, h, up_send.at[up, h], above).start()
         if down is not None:
             @pl.when(place > 0)
             def _():
-                weight_copy(slot, down_send.at[down], below).start()
-        weight_copy(slot, core_send.at[lax.div(slot, 2)], twin).start()
-
-    pass_on(shard, 0, 0)
+                weight_copy(slot, h, down_send.at[down, h], below).start()
+        weight_copy(slot, h, core_send.at[lax.div(slot, 2), h], twin).start()
+
+    def pass_own(h, carry):
+        pass_on(shard, h, 0, 0)
+        return carry
+
+    lax.fori_loop(0, SLICES, pass_own, 0)
+
+    units = groups * (width // SPAN)
+
+    def noise_copy(u):
+        per = width // SPAN
+        cs = pl.ds(pl.multiple_of(lax.rem(u, per) * SPAN, SPAN), SPAN)
+        return pltpu.make_async_copy(
+            stage.at[lax.rem(u, 2)],
+            noise_out.at[lax.div(u, per), :, cs],
+            noise_sem.at[lax.rem(u, 2)],
+        )
+
+    seed = seed_step[0]
+    key = seed_step[1] * 374761393
+
+    def noise_unit(u, carry):
+        per = width // SPAN
+        slot = lax.rem(u, 2)
+
+        @pl.when(u >= 2)
+        def _():
+            noise_copy(u - 2).wait()
+
+        base = (lax.div(u, per) * in_width + shard * rows) * width + lax.rem(u, per) * SPAN
+
+        def some_rows(r, inner):
+            index = (
+                lax.broadcasted_iota(jnp.int32, (32, SPAN), 0) * width
+                + lax.broadcasted_iota(jnp.int32, (32, SPAN), 1)
+                + (base + r * 32 * width)
+            )
+            count = noise_count(index, seed, key)
+            stage[slot, pl.ds(pl.multiple_of(r * 32, 32), 32), :] = count.astype(jnp.int16)
+            return inner
+
+        lax.fori_loop(0, rows // 32, some_rows, 0)
+        noise_copy(u).start()
+        return carry
 
     take_resid.wait()
 
@@ -119,17 +172,17 @@
     take_cot = pltpu.make_async_copy(cotangent, back, local_sem.at[0])
     take_cot.start()
 
-    def multiply(slot):
+    def multiply(slot, h):
         lhs = attn[:, pl.ds(pl.multiple_of(slot * rows, rows), rows)]
 
         def columns(j, carry):
-            sl = pl.ds(pl.multiple_of(j * 512, 512), 512)
+            sl = pl.ds(pl.multiple_of(h * piece_width + j * 512, 512), 512)
             total[:, sl] += jnp.dot(lhs, weights[slot, :, sl], preferred_element_type=jnp.float32)
             return carry
 
-        lax.fori_loop(0, width // 512, columns, 0)
-
-    def multiply_all(slots):
+        lax.fori_loop(0, piece_width // 512, columns, 0)
+
+    def multiply_all(slots, h):
         def one(i, carry):
             slot = slots[-1][0]
             for k in range(len(slots) - 1):
@@ -143,16 +196,21 @@
             def _():
                 @pl.when(from_twin)
                 def _():
-                    wait_weight(slot)
-                multiply(slot)
+                    wait_weight(slot, h)
+                multiply(slot, h)
             return carry
 
         lax.fori_loop(0, len(slots), one, 0)
 
     always = place >= 0
-    multiply_all([(shard, always), (twin, always)])
-
-    def gather_step(t, carry):
+
+    def multiply_own(h, carry):
+        multiply_all([(shard, always), (twin, always)], h)
+        return carry
+
+    def gather_step(i, carry):
+        t = lax.div(i, SLICES)
+        h = lax.rem(i, SLICES)
         low = place - 1 - t
         high = place + 1 + t
         low_slot = jnp.maximum(low, 0) * 2 + core
@@ -160,37 +218,53 @@
 
         @pl.when(low >= 0)
         def _():
-            wait_weight(low_slot)
-            pass_on(low_slot, t + 1, None)
+            wait_weight(low_slot, h)
+            pass_on(low_slot, h, t + 1, None)
 
         @pl.when(high <= last)
         def _():
-            wait_weight(high_slot)
-            pass_on(high_slot, None, t + 1)
-
+            wait_weight(high_slot, h)
+            pass_on(high_slot, h, None, t + 1)
+
+        @pl.when(i == 0)
+        def _():
+            lax.fori_loop(0, SLICES, multiply_own, 0)
+
+        steps = last * SLICES - 1
+        lax.fori_loop(
+            lax.div(units * jnp.minimum(i, steps), steps),
+            lax.div(units * jnp.minimum(i + 1, steps), steps),
+            noise_unit,
+            0,
+        )
         multiply_all([
             (low_slot, low >= 0),
             (high_slot, high <= last),
             (low_slot + 1 - 2 * core, low >= 0),
             (high_slot + 1 - 2 * core, high <= last),
-        ])
-        return carry
-
-    lax.fori_loop(0, last, gather_step, 0)
-
-    def drain_weights(t, carry):
+        ], h)
+        return carry
+
+    lax.fori_loop(0, last * SLICES, gather_step, 0)
+    noise_copy(units - 2).wait()
+    noise_copy(units - 1).wait()
+
+    def drain_weights(i, carry):
+        t = lax.div(i, SLICES)
+        h = lax.rem(i, SLICES)
+
         @pl.when((place < last) & (place - t >= 0))
         def _():
-            weight_copy(shard, up_send.at[t], above).wait_send()
+            weight_copy(shard, h, up_send.at[t, h], above).wait_send()
 
         @pl.when((place > 0) & (place + t <= last))
         def _():
-            weight_copy(shard, down_send.at[t], below).wait_send()
-
-        weight_copy(shard, core_send.at[t], twin).wait_send()
-        return carry
-
-    lax.fori_loop(0, line, drain_weights, 0)
+            weight_copy(shard, h, down_send.at[t, h], below).wait_send()
+
+        weight_copy(shard, h, core_send.at[t, h], twin).wait_send()
+        return carry
+
+    lax.fori_loop(0, line * SLICES, drain_weights, 0)
 
     take_cot.wait()
     span = 512
@@ -372,7 +446,7 @@
     lax.fori_loop(0, PIECES, finish, 0)
 
 
-def exchange(attn, resid, cotangent, gain, sampled, scaling):
+def exchange(seed_step, attn, resid, cotangent, gain, sampled, scaling):
     line = lax.axis_size("fsdp") // 2
     groups = lax.axis_size("sample")
     tokens, width = resid.shape
@@ -383,9 +457,12 @@
     dma = pltpu.SemaphoreType.DMA
     return pl.pallas_call(
         functools.partial(exchange_kernel, line, groups, scaling),
-        out_shape=jax.ShapeDtypeStruct((groups, rows, width), jnp.bfloat16),
-        in_specs=[vmem, vmem, vmem, hbm, hbm, hbm],
-        out_specs=hbm,
+        out_shape=(
+            jax.ShapeDtypeStruct((groups, rows, width), jnp.bfloat16),
+            jax.ShapeDtypeStruct((groups, rows, width), jnp.int16),
+        ),
+        in_specs=[pl.BlockSpec(memory_space=pltpu.SMEM), vmem, vmem, vmem, hbm, hbm, hbm],
+        out_specs=(hbm, hbm),
         scratch_shapes=[
             pltpu.VMEM((2 * line, rows, width), jnp.bfloat16),
             pltpu.VMEM((tokens, width), jnp.bfloat16),
@@ -393,11 +470,13 @@
             pltpu.VMEM((line, PIECES, rows, part), jnp.bfloat16),
             pltpu.VMEM((line + 1, PIECES, rows, part), jnp.bfloat16),
             pltpu.VMEM((PIECES, rows, part), jnp.bfloat16),
+            pltpu.VMEM((2, rows, SPAN), jnp.int16),
             dma((2,)),
-            dma((2 * line,)),
-            dma((line,)),
-            dma((line,)),
-            dma((line,)),
+            dma((2,)),
+            dma((2 * line, SLICES)),
+            dma((line, SLICES)),
+            dma((line, SLICES)),
+            dma((line, SLICES)),
             dma((line, PIECES)),
             dma((line, PIECES)),
             dma((line, PIECES)),
@@ -408,7 +487,7 @@
         compiler_params=pltpu.CompilerParams(
             collective_id=0, has_side_effects=True, vmem_limit_bytes=60 * 2**20
         ),
-    )(attn, attn.T, gain.astype(jnp.float32)[None, :], sampled, resid, cotangent)
+    )(seed_step, attn, attn.T, gain.astype(jnp.float32)[None, :], sampled, resid, cotangent)
 
 
 def per_device(seed_step, attn, resid, cotangent, gain, mean, hess, momentum):
@@ -425,12 +504,12 @@
         mean.astype(jnp.bfloat16).astype(jnp.float32)
         + sigma.astype(jnp.bfloat16).astype(jnp.float32) * epsilon
     ).astype(jnp.bfloat16)
-    grads = exchange(attn, resid, cotangent, gain, sampled, scaling)
+    grads, counts = exchange(seed_step, attn, resid, cotangent, gain, sampled, scaling)
     grad_sum = jnp.zeros((own_rows, width), jnp.float32)
     curv_sum = jnp.zeros((own_rows, width), jnp.float32)
     for g in range(groups):
         grad = grads[g].astype(jnp.float32)
-        noise = noise_table(seed_step, g, row_start, own_rows, in_width, width)
+        noise = noise_scale * ((counts[g].astype(jnp.float32) + 1.0) / 4096.0 - 1.0)
         grad_sum = grad_sum + grad
         curv_sum = curv_sum + grad * noise
     return ivon_update(mean, hess, momentum, grad_sum, curv_sum / sigma, groups)

time: 361 us -> 338 us (0.936)
  Pallas kernels: 322 us -> 306 us
  other arithmetic: 34.3 us -> 26.4 us
    pallas_call x1, Pallas kernels: 322 us -> 306 us  [exchange(): pl.pallas_call(functools.partial(exchange_kernel, line, groups, scaling),...]
    sub x1, other arithmetic: 24.9 us -> 17.4 us  [ivon_update(): mean - step_size * (new_momentum + damping * mean) / (new_hess + damping)]
where the time goes in v3:
time: 338 us
  Pallas kernels  306 us (91%)
  other arithmetic  26.4 us (8%)
  local copies, waits for them, and re-layouts  3.81 us (1%)
    pallas_call x1, Pallas kernels, exchange(): pl.pallas_call(functools.partial(exchange_kernel, line, groups, scaling),...  306 us
    sub x1, other arithmetic, ivon_update(): mean - step_size * (new_momentum + damping * mean) / (new_hess + damping)  17.4 us
    convert_element_type x1, other arithmetic, per_device(): sampled = (mean.astype(jnp.bfloat16).astype(jnp.float32) + sigma.astype(j...  7.74 us

profile of v3, /device:TPU:0, one launch (start us, length us, event | category | flops | bytes accessed | tf_op | source)
XLA Modules:
  0.0 338.0 jit_solution(10610599073553150322)
XLA Ops:
  0.6 1.3 fusion.10
  2.6 1.3 broadcast_in_dim.9
  3.9 0.0 copy-start
  3.9 7.7 %add_convert_fusion.sampled = bf16[256,4096]{1,0:T(8,128)(2,1)} fusion(f32[256,4096]{1,0:T(8,128)} %param.14, s32[]{:T(128)} %bitcast.3, s32[]{:T(128)} %bitcast.2, s32[256]{0:T(256)S(1)} %add_multiply_fusion, f32[256,4096]{1,0:T(8,128)} %param.13), kind=kLoop, calls=%fused_computation.17 | loop fusion | flops 34603008 | bytes 10486792 | tf_op jit(solution)/shard_map/convert_element_type | solution.py:506
  11.7 0.0 copy-done
  11.7 2.5 copy.11
  14.2 306.5 %shard_map.103 = (bf16[4,256,4096]{2,1,0:T(8,128)(2,1)}, s16[4,256,4096]{2,1,0:T(8,128)(2,1)}) custom-call(s32[2]{0:T(128)} %seed_step.1, bf16[512,2048]{1,0:T(8,128)(2,1)} %attn.1, bf16[2048,512]{1,0:T(8,128)(2,1)} %bitcast.16, f32[1,4096]{1,0:T(1,128)} %bitcast.17, bf16[256,4096]{1,0:T(8,128)(2,1)} %add_convert_fusion.sampled, bf16[512,4096]{1,0:T(8,128)(2,1)} %resid.1, ...), custom_call_target="tpu_custom_call" | custom-call | tf_op jit(solution)/shard_map/pallas_call | solution.py:458
  320.6 17.4 %divide_subtract_fusion = (f32[256,4096]{1,0:T(8,128)}, f32[256,4096]{1,0:T(8,128)}, f32[256,4096]{1,0:T(8,128)}) fusion(f32[256,4096]{1,0:T(8,128)} %param.13, bf16[4,256,4096]{2,1,0:T(8,128)(2,1)} %get-tuple-element.5, f32[256,4096]{1,0:T(8,128)} %param.15, f32[256,4096]{1,0:T(8,128)} %param.14, s16[4,256,4096]{2,1,0:T(8,128)(2,1)} %get-tuple-element.6), kind=kLoop, calls=%fused_computation.15 | loop fusion | flops 57671680 | bytes 41943040 | tf_op jit(solution)/shard_map/sub | solution.py:49
  (1 shorter events, 0.0 us)
Async XLA Ops:
  3.9 7.7 %copy-start = (bf16[512,2048]{1,0:T(8,128)(2,1)S(1)}, bf16[512,2048]{1,0:T(8,128)(2,1)}, u32[]{:S(2)}) copy-start(bf16[512,2048]{1,0:T(8,128)(2,1)} %attn.1) | copy-start | bytes 6291460

commit v4 on v3

--- a/solution.py
+++ b/solution.py
@@ -58,7 +58,7 @@
 
 def exchange_kernel(
     line, groups, scaling,
-    seed_step, attn, attn_t, gain, sampled, resid, cotangent, out, noise_out,
+    seed_step, attn, gain, sampled, resid, cotangent, out, noise_out,
     weights, back, total, paired, chained, ready, stage,
     noise_sem, local_sem, weight_recv, up_send, down_send, core_send,
     pair_send, pair_recv, chain_send, chain_recv, group_send, group_recv,
@@ -293,9 +293,12 @@
     lax.fori_loop(0, tokens // 16, normalise, 0)
 
     def partial(block, piece):
-        lhs = attn_t[pl.ds(pl.multiple_of(block * rows, rows), rows), :]
+        lhs = attn[:, pl.ds(pl.multiple_of(block * rows, rows), rows)]
         rhs = back[:, pl.ds(pl.multiple_of(piece * part, part), part)]
-        return jnp.dot(lhs, rhs, preferred_element_type=jnp.float32) * scaling
+        return (
+            lax.dot_general(lhs, rhs, (((0,), (0,)), ((), ())), preferred_element_type=jnp.float32)
+            * scaling
+        )
 
     def pair_copy(goal, piece):
         return pltpu.make_async_remote_copy(
@@ -336,10 +339,11 @@
 
         @pl.when(jnp.logical_not(first))
         def _():
+            term = own_term(goal, piece)
             chain_copy(goal, goal, piece, other).wait_recv()
-            chained[goal, piece] = (
-                own_term(goal, piece) + chained[goal, piece].astype(jnp.float32)
-            ).astype(jnp.bfloat16)
+            chained[goal, piece] = (term + chained[goal, piece].astype(jnp.float32)).astype(
+                jnp.bfloat16
+            )
 
         chain_copy(goal, slot, piece, other).start()
 
@@ -397,6 +401,7 @@
         @pl.when((lax.rem(step, last) == 0) & (turn >= 1))
         def _():
             piece = turn - 1
+            term = own_term(place, piece)
 
             @pl.when(place > 0)
             def _():
@@ -407,7 +412,7 @@
                 chain_copy(place, line, piece, above).wait_recv()
 
             ready[piece] = (
-                own_term(place, piece)
+                term
                 + chained[place, piece].astype(jnp.float32)
                 + chained[line, piece].astype(jnp.float32)
             ).astype(jnp.bfloat16)
@@ -461,7 +466,7 @@
             jax.ShapeDtypeStruct((groups, rows, width), jnp.bfloat16),
             jax.ShapeDtypeStruct((groups, rows, width), jnp.int16),
         ),
-        in_specs=[pl.BlockSpec(memory_space=pltpu.SMEM), vmem, vmem, vmem, hbm, hbm, hbm],
+        in_specs=[pl.BlockSpec(memory_space=pltpu.SMEM), vmem, vmem, hbm, hbm, hbm],
         out_specs=(hbm, hbm),
         scratch_shapes=[
             pltpu.VMEM((2 * line, rows, width), jnp.bfloat16),
@@ -487,7 +492,7 @@
         compiler_params=pltpu.CompilerParams(
             collective_id=0, has_side_effects=True, vmem_limit_bytes=60 * 2**20
         ),
-    )(seed_step, attn, attn.T, gain.astype(jnp.float32)[None, :], sampled, resid, cotangent)
+    )(seed_step, attn, gain.astype(jnp.float32)[None, :], sampled, resid, cotangent)
 
 
 def per_device(seed_step, attn, resid, cotangent, gain, mean, hess, momentum):

time: 338 us -> 335 us (level)
  no operation moved by 1% of the time
where the time goes in v4:
time: 335 us
  Pallas kernels  306 us (91%)
  other arithmetic  26.3 us (8%)
    pallas_call x1, Pallas kernels, exchange(): pl.pallas_call(functools.partial(exchange_kernel, line, groups, scaling),...  306 us
    sub x1, other arithmetic, ivon_update(): mean - step_size * (new_momentum + damping * mean) / (new_hess + damping)  17.4 us
    convert_element_type x1, other arithmetic, per_device(): sampled = (mean.astype(jnp.bfloat16).astype(jnp.float32) + sigma.astype(j...  7.59 us

profile of v4, /device:TPU:0, one launch (start us, length us, event | category | flops | bytes accessed | tf_op | source)
XLA Modules:
  0.0 334.8 jit_solution(16848809393575919317)
XLA Ops:
  0.6 1.3 fusion.10
  2.6 1.3 broadcast_in_dim.9
  3.9 7.6 %add_convert_fusion.sampled = bf16[256,4096]{1,0:T(8,128)(2,1)} fusion(f32[256,4096]{1,0:T(8,128)} %param.14, s32[]{:T(128)} %bitcast.2, s32[]{:T(128)} %bitcast.1, s32[256]{0:T(256)S(1)} %add_multiply_fusion, f32[256,4096]{1,0:T(8,128)} %param.13), kind=kLoop, calls=%fused_computation.17 | loop fusion | flops 34603008 | bytes 10486792 | tf_op jit(solution)/shard_map/convert_element_type | solution.py:511
  11.5 305.8 %shard_map.103 = (bf16[4,256,4096]{2,1,0:T(8,128)(2,1)}, s16[4,256,4096]{2,1,0:T(8,128)(2,1)}) custom-call(s32[2]{0:T(128)} %seed_step.1, bf16[512,2048]{1,0:T(8,128)(2,1)} %attn.1, f32[1,4096]{1,0:T(1,128)} %bitcast.15, bf16[256,4096]{1,0:T(8,128)(2,1)} %add_convert_fusion.sampled, bf16[512,4096]{1,0:T(8,128)(2,1)} %resid.1, bf16[512,4096]{1,0:T(8,128)(2,1)} %cotangent.1), custom_call_target="tpu_custom_call" | custom-call | tf_op jit(solution)/shard_map/pallas_call | solution.py:463
  317.4 17.4 %divide_subtract_fusion = (f32[256,4096]{1,0:T(8,128)}, f32[256,4096]{1,0:T(8,128)}, f32[256,4096]{1,0:T(8,128)}) fusion(f32[256,4096]{1,0:T(8,128)} %param.13, bf16[4,256,4096]{2,1,0:T(8,128)(2,1)} %get-tuple-element.5, f32[256,4096]{1,0:T(8,128)} %param.15, f32[256,4096]{1,0:T(8,128)} %param.14, s16[4,256,4096]{2,1,0:T(8,128)(2,1)} %get-tuple-element.6), kind=kLoop, calls=%fused_computation.15 | loop fusion | flops 57671680 | bytes 41943040 | tf_op jit(solution)/shard_map/sub | solution.py:49
  (1 shorter events, 0.0 us)
